TPU v7x, 256 devices: a whole 4x4x8 slice. The times are simulated.
256 devices in a mesh: replica: 16 (over z_lo, x), fsdp: 16 (over y, z_hi, core).
Axes of the slice: x: 4, y: 4, z: 8 (z_hi: 2, z_lo: 4; z = z_hi * 4 + z_lo), core: 2. Of those that a mesh axis runs over, the one named last changes fastest.
Arguments:
- base: float32 [8192, 1024], P('fsdp'), may hold values from -6 to 6
- local: bfloat16 [16, 8192, 1024], P('replica', 'fsdp'), may hold values from -6 to 6
- momentum: float32 [8192, 1024], P('fsdp'), may hold values from -6 to 6
- tokens: bfloat16 [16, 2048, 8192], P('replica', 'fsdp'), may hold values from -6 to 6
- mask_embed: bfloat16 [8192], replicated, may hold values from -6 to 6
- mask_pos: int32 [16, 1, 768], P('replica'), may hold values from 0 to 2047, as said below
- cotangent: bfloat16 [16, 2048, 1024], P('replica', 'fsdp'), may hold values from -6 to 6
Outputs:
- new_momentum: bfloat16 [8192, 1024], P('fsdp')
- stepped: bfloat16 [16, 8192, 1024], P('replica', 'fsdp')
Inputs may be any that keep to these rules, and one draw needn't show every extreme that they name: `mask_pos`: each row holds 768 different positions of its sequence.
All inputs are finite; a program needn't handle non-finite values. Where the computation divides by a largest or mean magnitude, that divisor is 1e-20 or more.
Results may differ from a plain program's by a relative error of at most 0.008.
Values may be sent and summed in bfloat16 or wider, within the bound.
A program may use at most 128 MiB of HBM per device.

v0:
```python
import jax
import jax.numpy as jnp
from jax import lax
from jax.sharding import PartitionSpec as P

D = 8192
QBLOCK = 128
LENGTH = 2048
momentum_decay = 0.9
outer_rate = 0.7
inner_rate = 0.5


def body(base, local, momentum, tokens, mask_embed, mask_pos, cotangent):
    row_count, col_count = base.shape
    drift = base - local[0].astype(jnp.float32)
    blocks = drift.reshape(row_count, col_count // QBLOCK, QBLOCK)
    scales = (jnp.max(jnp.abs(blocks), axis=2, keepdims=True) + 1e-06).astype(jnp.bfloat16)
    code_vals = (blocks / scales.astype(jnp.float32)).astype(jnp.bfloat16)
    replicas = lax.axis_size("replica")
    dequant = (code_vals.astype(jnp.float32) * scales.astype(jnp.float32)).reshape(
        row_count, col_count
    )
    outer_grad = lax.psum(dequant, "replica") / replicas
    momentum_next = momentum_decay * momentum + outer_grad
    renewed = base - outer_rate * (outer_grad + momentum_decay * momentum_next)
    tok_rows = tokens.shape[1]
    offset = lax.axis_index("fsdp") * tok_rows
    places = offset + jnp.arange(tok_rows, dtype=jnp.int32)
    sequence = places // LENGTH
    position = places % LENGTH
    seq_ids = jnp.arange(mask_pos.shape[1], dtype=jnp.int32)
    matches = (mask_pos[0][None, :, :] == position[:, None, None]) & (
        sequence[:, None, None] == seq_ids[None, :, None]
    )
    masked = jnp.any(matches, axis=(1, 2))
    inputs = jnp.where(masked[:, None], mask_embed[None, :], tokens[0])
    upstream = cotangent[0]
    own_columns = lax.all_to_all(inputs, "fsdp", split_axis=1, concat_axis=0, tiled=True)
    all_upstream = lax.all_gather(upstream, "fsdp", axis=0, tiled=True)
    groups = lax.axis_size("fsdp")
    group_in = own_columns.reshape(groups, tok_rows, row_count)
    group_up = all_upstream.reshape(groups, tok_rows, col_count)

    def add_group(total, pair):
        term = lax.dot_general(
            pair[0], pair[1], (((0,), (0,)), ((), ())), preferred_element_type=jnp.float32
        )
        return (total + term.astype(jnp.bfloat16).astype(jnp.float32), None)

    grad_sum, _ = lax.scan(
        add_group, jnp.zeros((row_count, col_count), jnp.float32), (group_in, group_up)
    )
    gradient = grad_sum * D ** (-0.5)
    stepped = (renewed - inner_rate * gradient).astype(jnp.bfloat16)
    return (momentum_next.astype(jnp.bfloat16), stepped[None])


def solution(mesh):
    in_specs = (
        P("fsdp", None),
        P("replica", "fsdp", None),
        P("fsdp", None),
        P("replica", "fsdp", None),
        P(),
        P("replica", None, None),
        P("replica", "fsdp", None),
    )
    out_specs = (P("fsdp", None), P("replica", "fsdp", None))
    return jax.shard_map(body, mesh=mesh, in_specs=in_specs, out_specs=out_specs, check_vma=False)
```

profile of v0, /device:TPU:8, one launch (start us, length us, event | category | flops | bytes accessed | tf_op | source)
XLA Modules:
  0.0 255.8 jit_solution(18432817212518945594)
XLA Ops:
  8.0 0.0 all-gather.3.cloned.1.call-start
  8.0 0.7 all-gather.3.cloned.1.call-update
  8.7 0.0 copy-start.2
  8.7 0.0 copy-start.3
  8.8 3.2 %copy.18 = bf16[1,128,8192]{1,2,0:T(8,128)(2,1)S(1)} copy(bf16[1,128,8192]{2,1,0:T(8,128)(2,1)} %param.12) | data formatting | bytes 4194304 | tf_op args[3]
  12.0 0.0 copy-done.2
  12.0 0.0 copy-done.3
  12.1 0.2 and_reduce_fusion
  12.3 2.2 broadcast_select_fusion
  14.5 0.0 copy-start
  14.5 0.0 copy-start.1
  14.5 11.8 %all-to-all-start = ((bf16[128,16,512]{0,2,1:T(8,128)(2,1)}), bf16[128,16,512]{0,2,1:T(8,128)(2,1)}, u32[]{:S(2)}, u32[]{:S(2)}) async-start(bf16[128,16,512]{0,2,1:T(8,128)(2,1)} %broadcast_select_fusion), calls=%async_computation | async-start | bytes 4194304 | tf_op jit(solution)/shard_map/all_to_all | solution.py:39
  26.4 0.0 all-reduce.2.cloned.1.call-start
  26.4 0.0 copy-done
  26.4 0.0 copy-done.1
  26.4 0.3 abs_bitcast_fusion
  26.8 1.8 copy.21
  28.6 2.2 reduce_max.9
  30.8 0.1 copy.16
  30.9 0.1 copy.17
  31.1 0.6 div.29
  31.7 2.1 bitcast_multiply_fusion
  33.8 0.0 all-reduce.2.cloned.1.call-update
  33.9 46.6 %all-to-all-done = bf16[128,16,512]{0,2,1:T(8,128)(2,1)} async-done(((bf16[128,16,512]{0,2,1:T(8,128)(2,1)}), bf16[128,16,512]{0,2,1:T(8,128)(2,1)}, u32[]{:S(2)}, u32[]{:S(2)}) %all-to-all-start) | async-done | bytes 2097184 | tf_op jit(solution)/shard_map/all_to_all | solution.py:39
  80.4 41.1 %all-gather.3.cloned.1.call-done = bf16[1,2048,1024]{2,1,0:T(8,128)(2,1)} async-done(((bf16[1,128,1024]{2,1,0:T(8,128)(2,1)}), bf16[1,2048,1024]{2,1,0:T(8,128)(2,1)}) %all-gather.3.cloned.1.call-update) | async-done | bytes 4194320 | tf_op jit(solution)/shard_map/all_gather | solution.py:40
  121.5 27.8 %while.11 = (s32[]{:T(128)}, f32[512,1024]{1,0:T(8,128)S(1)}, bf16[16,128,512]{1,2,0:T(8,128)(2,1)}, bf16[16,128,1024]{2,1,0:T(8,128)(2,1)}, s32[]{:T(128)}, /*index=5*/s32[]{:T(128)}) while((s32[]{:T(128)}, f32[512,1024]{1,0:T(8,128)S(1)}, bf16[16,128,512]{1,2,0:T(8,128)(2,1)}, bf16[16,128,1024]{2,1,0:T(8,128)(2,1)}, s32[]{:T(128)}, ...), condition=%wide.region_4.5_spmd.clone, body=%wide.region_3.4_spmd.clone.sunk | while | flops 136314880 | bytes 4588623 | solution.py:51
  121.5 1.7 select_add_fusion.2
  123.3 1.7 select_add_fusion.2
  125.0 1.7 select_add_fusion.2
  126.7 1.7 select_add_fusion.2
  128.5 1.7 select_add_fusion.2
  130.2 1.7 select_add_fusion.2
  132.0 1.7 select_add_fusion.2
  133.7 1.7 select_add_fusion.2
  135.4 1.7 select_add_fusion.2
  137.2 1.7 select_add_fusion.2
  138.9 1.7 select_add_fusion.2
  140.7 1.7 select_add_fusion.2
  142.4 1.7 select_add_fusion.2
  144.1 1.7 select_add_fusion.2
  145.9 1.7 select_add_fusion.2
  147.6 1.7 select_add_fusion.2
  149.4 93.7 %all-reduce.2.cloned.1.call-done = f32[512,1024]{1,0:T(8,128)} async-done(((f32[512,1024]{1,0:T(8,128)}), f32[512,1024]{1,0:T(8,128)}) %all-reduce.2.cloned.1.call-update) | async-done | bytes 2097168 | tf_op jit(solution)/shard_map/psum | solution.py:24
  243.1 5.3 %fusion.7 = (bf16[1,512,1024]{2,1,0:T(8,128)(2,1)}, bf16[512,1024]{1,0:T(8,128)(2,1)}) fusion(f32[512,1024]{1,0:T(8,128)S(1)} %get-tuple-element.24, f32[512,1024]{1,0:T(8,128)} %param.9, f32[512,1024]{1,0:T(8,128)} %param.11, f32[512,1024]{1,0:T(8,128)} %all-reduce.2.cloned.1.call-done), kind=kLoop, calls=%fused_computation.16 | loop fusion | flops 5767168 | bytes 10485760 | tf_op jit(solution)/shard_map/broadcast_in_dim | solution.py:56
  (6 shorter events, 0.1 us)
Async XLA Ops:
  8.0 113.5 %all-gather.3.cloned.1.call-start = ((), (), s32[]{:S(2)}) async-start(), calls=%async_computation.2 | async-start | bytes 4456448 | tf_op jit(solution)/shard_map/all_gather | solution.py:40
  8.7 3.3 %copy-start.2 = (bf16[8192]{0:T(1024)(128)(2,1)S(1)}, bf16[8192]{0:T(1024)(128)(2,1)}, u32[]{:S(2)}) copy-start(bf16[8192]{0:T(1024)(128)(2,1)} %param.13) | copy-start | bytes 49156
  8.7 3.3 %copy-start.3 = (s32[1,1,768]{2,1,0:T(1,128)S(1)}, s32[1,1,768]{2,1,0:T(1,128)}, u32[]{:S(2)}) copy-start(s32[1,1,768]{2,1,0:T(1,128)} %param.14) | copy-start | bytes 9220
  14.5 11.9 %copy-start = (f32[512,1024]{1,0:T(8,128)S(1)}, f32[512,1024]{1,0:T(8,128)}, u32[]{:S(2)}) copy-start(f32[512,1024]{1,0:T(8,128)} %param.9) | copy-start | bytes 6291460
  14.5 11.9 %copy-start.1 = (bf16[1,512,1024]{2,1,0:T(8,128)(2,1)S(1)}, bf16[1,512,1024]{2,1,0:T(8,128)(2,1)}, u32[]{:S(2)}) copy-start(bf16[1,512,1024]{2,1,0:T(8,128)(2,1)} %param.10) | copy-start | bytes 3145732
  14.5 65.9 %all-to-all-start = ((bf16[128,16,512]{0,2,1:T(8,128)(2,1)}), bf16[128,16,512]{0,2,1:T(8,128)(2,1)}, u32[]{:S(2)}, u32[]{:S(2)}) async-start(bf16[128,16,512]{0,2,1:T(8,128)(2,1)} %broadcast_select_fusion), calls=%async_computation | async-start | bytes 4194304 | tf_op jit(solution)/shard_map/all_to_all | solution.py:39
  26.4 216.7 %all-reduce.2.cloned.1.call-start = ((), (), s32[]{:S(2)}) async-start(), calls=%async_computation.1 | async-start | bytes 4194304 | tf_op jit(solution)/shard_map/psum | solution.py:24
Sparse Core Ops, SparseCore 0:
  11.5 109.9 all-gather.2
Sparse Core Ops, SparseCore 1:
  33.9 209.1 all-reduce.1
where the time goes:
time: 256 us
  waiting for transfers between devices  182 us (71%)
  matrix products  27.5 us (11%)
  between operations  15.6 us (6%)
  other arithmetic  12.4 us (5%)
  starting transfers between devices  11.9 us (5%)
  local copies, waits for them, and re-layouts  5.93 us (2%)
    psum x1, waiting for transfers between devices, body(): outer_grad = lax.psum(dequant, 'replica') / replicas  93.7 us
    all_to_all x1, waiting for transfers between devices, body(): lax.all_to_all(inputs, 'fsdp', split_axis=1, concat_axis=0, tiled=True)  46.6 us
    all_gather x1, waiting for transfers between devices, body(): all_upstream = lax.all_gather(upstream, 'fsdp', axis=0, tiled=True)  41.1 us
    dot_general x16, matrix products, add_group(): lax.dot_general(pair[0], pair[1], (((0,), (0,)), ((), ())), preferred_ele...  27.5 us
    all_to_all x1, starting transfers between devices, body(): lax.all_to_all(inputs, 'fsdp', split_axis=1, concat_axis=0, tiled=True)  11.8 us
    broadcast_in_dim x1, other arithmetic, body(): return (momentum_next.astype(jnp.bfloat16), stepped[None])  5.25 us
  transfers between devices with their start and end apart: 3, of which 3 were waited for; matrix products, arithmetic and copies ran while one was open for 16% of the time, Pallas kernels for 0%

commit v1 on v0

--- a/solution.py
+++ b/solution.py
@@ -37,7 +37,13 @@
     inputs = jnp.where(masked[:, None], mask_embed[None, :], tokens[0])
     upstream = cotangent[0]
     own_columns = lax.all_to_all(inputs, "fsdp", split_axis=1, concat_axis=0, tiled=True)
-    all_upstream = lax.all_gather(upstream, "fsdp", axis=0, tiled=True)
+    _extend_heads = lambda chunk, peer_axis: jnp.concatenate(
+        lax.all_to_all(
+            jnp.stack([chunk for _ in range(lax.psum(1, peer_axis))], axis=0), peer_axis, 0, 0
+        ),
+        0,
+    )
+    all_upstream = _extend_heads(upstream, peer_axis="fsdp")
     groups = lax.axis_size("fsdp")
     group_in = own_columns.reshape(groups, tok_rows, row_count)
     group_up = all_upstream.reshape(groups, tok_rows, col_count)

time: 256 us -> 311 us (1.21)
  blocking collectives: 0 us -> 51.2 us
  starting transfers between devices: 11.9 us -> 18.5 us
  waiting for transfers between devices: 182 us -> 178 us
    all_to_all x0 -> x1, blocking collectives: none -> 51.2 us  [body(): lax.all_to_all(inputs, 'fsdp', split_axis=1, concat_axis=0, tiled=True)]
    all_gather x1 -> x0, waiting for transfers between devices: 41.1 us -> none  [body(): all_upstream = lax.all_gather(upstream, 'fsdp', axis=0, tiled=True)]
    psum x1, waiting for transfers between devices: 93.7 us -> 123 us  [body(): outer_grad = lax.psum(dequant, 'replica') / replicas]
    all_to_all x1, waiting for transfers between devices: 46.6 us -> 55.4 us  [body(): lax.all_to_all(jnp.stack([chunk for _ in range(lax.psum(1, peer_axis))],...]
    all_to_all x1, starting transfers between devices: 11.8 us -> 18.4 us  [body(): lax.all_to_all(jnp.stack([chunk for _ in range(lax.psum(1, peer_axis))],...]
  transfers between devices with their start and end apart: 3 -> 2, of which waited for: 3 -> 2; matrix products, arithmetic and copies ran while one was open for 16% -> 11% of each run, Pallas kernels for 0% -> 0%
where the time goes in v1:
time: 311 us; the launch traced here: 310 us
  waiting for transfers between devices  178 us (57%)
  blocking collectives  51.2 us (16%)
  matrix products  27.5 us (9%)
  starting transfers between devices  18.5 us (6%)
  between operations  14.2 us (5%)
  other arithmetic  11.7 us (4%)
  local copies, waits for them, and re-layouts  8.38 us (3%)
    psum x1, waiting for transfers between devices, body(): outer_grad = lax.psum(dequant, 'replica') / replicas  123 us
    all_to_all x1, waiting for transfers between devices, body(): lax.all_to_all(jnp.stack([chunk for _ in range(lax.psum(1, peer_axis))],...  55.4 us
    all_to_all x1, blocking collectives, body(): lax.all_to_all(inputs, 'fsdp', split_axis=1, concat_axis=0, tiled=True)  51.2 us
    dot_general x16, matrix products, add_group(): lax.dot_general(pair[0], pair[1], (((0,), (0,)), ((), ())), preferred_ele...  27.5 us
    all_to_all x1, starting transfers between devices, body(): lax.all_to_all(jnp.stack([chunk for _ in range(lax.psum(1, peer_axis))],...  18.4 us
  transfers between devices with their start and end apart: 2, of which 2 were waited for; matrix products, arithmetic and copies ran while one was open for 11% of the time, Pallas kernels for 0%

profile of v1, /device:TPU:8, one launch (start us, length us, event | category | flops | bytes accessed | tf_op | source)
XLA Modules:
  0.0 310.0 jit_solution(14918062218840260866)
XLA Ops:
  7.2 0.0 copy-start.3
  7.2 0.0 copy-start.4
  7.2 3.2 %copy.18 = bf16[1,128,8192]{1,2,0:T(8,128)(2,1)S(1)} copy(bf16[1,128,8192]{2,1,0:T(8,128)(2,1)} %param.12) | data formatting | bytes 4194304 | tf_op args[3]
  10.5 0.0 copy-done.3
  10.5 0.0 copy-done.4
  10.5 0.2 and_reduce_fusion
  10.7 1.5 broadcast_select_fusion
  12.2 0.0 copy-start.2
  12.2 51.2 %all_to_all.18 = bf16[128,16,512]{0,2,1:T(8,128)(2,1)} all-to-all(bf16[128,16,512]{0,2,1:T(8,128)(2,1)S(1)} %broadcast_select_fusion), channel_id=1, replica_groups=mesh['replica'=16,'fsdp'=16] {'fsdp'}, dimensions={1} | all-to-all | bytes 4194304 | tf_op jit(solution)/shard_map/all_to_all | solution.py:39
  63.4 0.0 copy-done.2
  63.4 2.5 stack.3
  65.9 0.0 copy-start
  65.9 0.0 copy-start.1
  65.9 18.4 %all-to-all-start.1 = ((bf16[16,128,1024]{2,1,0:T(8,128)(2,1)}), bf16[16,128,1024]{2,1,0:T(8,128)(2,1)}, u32[]{:S(2)}, u32[]{:S(2)}) async-start(bf16[16,128,1024]{2,1,0:T(8,128)(2,1)} %stack.3), calls=%async_computation.1 | async-start | bytes 8388608 | tf_op jit(solution)/shard_map/all_to_all | solution.py:41
  84.4 0.0 all-reduce.2.cloned.1.call-start
  84.4 0.0 copy-done
  84.4 0.0 copy-done.1
  84.4 0.3 abs_bitcast_fusion
  84.8 1.8 copy.21
  86.5 2.2 reduce_max.9
  88.8 0.1 copy.16
  88.9 0.1 copy.17
  89.0 0.6 div.29
  89.6 2.2 bitcast_multiply_fusion
  91.8 0.0 all-reduce.2.cloned.1.call-update
  91.8 55.4 %all-to-all-done.1 = bf16[16,128,1024]{2,1,0:T(8,128)(2,1)} async-done(((bf16[16,128,1024]{2,1,0:T(8,128)(2,1)}), bf16[16,128,1024]{2,1,0:T(8,128)(2,1)}, u32[]{:S(2)}, u32[]{:S(2)}) %all-to-all-start.1) | async-done | bytes 4194336 | tf_op jit(solution)/shard_map/all_to_all | solution.py:41
  147.3 27.8 %while.11 = (s32[]{:T(128)}, f32[512,1024]{1,0:T(8,128)S(1)}, bf16[16,128,512]{1,2,0:T(8,128)(2,1)}, bf16[16,128,1024]{2,1,0:T(8,128)(2,1)}, s32[]{:T(128)}, /*index=5*/s32[]{:T(128)}) while((s32[]{:T(128)}, f32[512,1024]{1,0:T(8,128)S(1)}, bf16[16,128,512]{1,2,0:T(8,128)(2,1)}, bf16[16,128,1024]{2,1,0:T(8,128)(2,1)}, s32[]{:T(128)}, ...), condition=%wide.region_4.5_spmd.clone, body=%wide.region_3.4_spmd.clone.sunk | while | flops 136314880 | bytes 4588623 | solution.py:57
  147.3 1.7 select_add_fusion.2
  149.0 1.7 select_add_fusion.2
  150.7 1.7 select_add_fusion.2
  152.5 1.7 select_add_fusion.2
  154.2 1.7 select_add_fusion.2
  156.0 1.7 select_add_fusion.2
  157.7 1.7 select_add_fusion.2
  159.5 1.7 select_add_fusion.2
  161.2 1.7 select_add_fusion.2
  162.9 1.7 select_add_fusion.2
  164.7 1.7 select_add_fusion.2
  166.4 1.7 select_add_fusion.2
  168.2 1.7 select_add_fusion.2
  169.9 1.7 select_add_fusion.2
  171.6 1.7 select_add_fusion.2
  173.4 1.7 select_add_fusion.2
  175.1 122.8 %all-reduce.2.cloned.1.call-done = f32[512,1024]{1,0:T(8,128)} async-done(((f32[512,1024]{1,0:T(8,128)}), f32[512,1024]{1,0:T(8,128)}) %all-reduce.2.cloned.1.call-update) | async-done | bytes 2097168 | tf_op jit(solution)/shard_map/psum | solution.py:24
  297.9 5.3 %fusion.7 = (bf16[1,512,1024]{2,1,0:T(8,128)(2,1)}, bf16[512,1024]{1,0:T(8,128)(2,1)}) fusion(f32[512,1024]{1,0:T(8,128)S(1)} %get-tuple-element.24, f32[512,1024]{1,0:T(8,128)} %param.9, f32[512,1024]{1,0:T(8,128)} %param.11, f32[512,1024]{1,0:T(8,128)} %all-reduce.2.cloned.1.call-done), kind=kLoop, calls=%fused_computation.16 | loop fusion | flops 5767168 | bytes 10485760 | tf_op jit(solution)/shard_map/broadcast_in_dim | solution.py:62
  (6 shorter events, 0.1 us)
Async XLA Ops:
  7.2 3.3 %copy-start.3 = (bf16[8192]{0:T(1024)(128)(2,1)S(1)}, bf16[8192]{0:T(1024)(128)(2,1)}, u32[]{:S(2)}) copy-start(bf16[8192]{0:T(1024)(128)(2,1)} %param.13) | copy-start | bytes 49156
  7.2 3.3 %copy-start.4 = (s32[1,1,768]{2,1,0:T(1,128)S(1)}, s32[1,1,768]{2,1,0:T(1,128)}, u32[]{:S(2)}) copy-start(s32[1,1,768]{2,1,0:T(1,128)} %param.14) | copy-start | bytes 9220
  12.2 51.2 %copy-start.2 = (bf16[1,128,1024]{2,1,0:T(8,128)(2,1)S(1)}, bf16[1,128,1024]{2,1,0:T(8,128)(2,1)}, u32[]{:S(2)}) copy-start(bf16[1,128,1024]{2,1,0:T(8,128)(2,1)} %param.15) | copy-start | bytes 786436
  65.9 18.5 %copy-start = (f32[512,1024]{1,0:T(8,128)S(1)}, f32[512,1024]{1,0:T(8,128)}, u32[]{:S(2)}) copy-start(f32[512,1024]{1,0:T(8,128)} %param.9) | copy-start | bytes 6291460
  65.9 18.5 %copy-start.1 = (bf16[1,512,1024]{2,1,0:T(8,128)(2,1)S(1)}, bf16[1,512,1024]{2,1,0:T(8,128)(2,1)}, u32[]{:S(2)}) copy-start(bf16[1,512,1024]{2,1,0:T(8,128)(2,1)} %param.10) | copy-start | bytes 3145732
  65.9 81.3 %all-to-all-start.1 = ((bf16[16,128,1024]{2,1,0:T(8,128)(2,1)}), bf16[16,128,1024]{2,1,0:T(8,128)(2,1)}, u32[]{:S(2)}, u32[]{:S(2)}) async-start(bf16[16,128,1024]{2,1,0:T(8,128)(2,1)} %stack.3), calls=%async_computation.1 | async-start | bytes 8388608 | tf_op jit(solution)/shard_map/all_to_all | solution.py:41
  84.4 213.6 %all-reduce.2.cloned.1.call-start = ((), (), s32[]{:S(2)}) async-start(), calls=%async_computation.2 | async-start | bytes 4194304 | tf_op jit(solution)/shard_map/psum | solution.py:24
Sparse Core Ops, SparseCore 0:
  91.9 205.9 all-reduce.1
